TPU v7x, 256 devices: a whole 4x4x8 slice. The times are simulated.
256 devices in a mesh: sp: 64 (over y, z, core), dp: 4 (over x).
Axes of the slice: x: 4, y: 4, z: 8, core: 2. Of those that a mesh axis runs over, the one named last changes fastest.
Arguments:
- volume: bfloat16 [4, 96, 256, 8, 128], P('dp', None, 'sp'), may hold values from -6 to 6
- cotangent: bfloat16 [4, 96, 256, 8, 128], P('dp', None, 'sp'), may hold values from -6 to 6
- kernels_xy: bfloat16 [2, 96, 3, 3], replicated, may hold values from -2 to 2
- kernels_z: bfloat16 [2, 96, 3], replicated, may hold values from -3.5 to 3.5
- mixing: bfloat16 [2, 96, 96], replicated, may hold values from -0.625 to 0.625
Outputs:
- volume_grad: bfloat16 [4, 96, 256, 8, 128], P('dp', None, 'sp')
- mixing_grad: float32 [2, 96, 96], replicated
- xy_grad: float32 [2, 96, 3, 3], replicated
- z_grad: float32 [2, 96, 3], replicated
All inputs are finite; a program needn't handle non-finite values.
Results may differ from a plain program's by a relative error of at most 0.018.
Values may be sent and summed in bfloat16 or wider, within the bound.
A program may use at most 64 MiB of HBM per device.

v0:
```python
import math
import jax
import jax.numpy as jnp
from jax import lax
from jax.sharding import PartitionSpec as P


def padded_2(x, sides, width):
    for axis, dim in sides:
        count, length = (lax.axis_size(axis), x.shape[dim])
        up = [(i, (i + 1) % count) for i in range(count - 1)]
        down = [(j, i) for i, j in up]
        last = lax.slice_in_dim(x, length - width, length, axis=dim)
        first = lax.slice_in_dim(x, 0, width, axis=dim)
        before = lax.ppermute(last, axis, up)
        after = lax.ppermute(first, axis, down)
        x = jnp.concatenate([before, x, after], axis=dim)
    return x


def conv_plane(inputs, kernel):
    extent = inputs.shape[1] - 2
    across = inputs.shape[3]
    padded = jnp.pad(inputs, ((0, 0), (0, 0), (0, 0), (1, 1)))
    summed = jnp.zeros((inputs.shape[0], extent, inputs.shape[2], across), jnp.float32)
    for row_tap in range(3):
        for col_tap in range(3):
            summed = summed + kernel[:, row_tap, col_tap][:, None, None, None] * padded[
                :, row_tap : row_tap + extent, :, col_tap : col_tap + across
            ].astype(jnp.float32)
    return summed


def conv_depth(inputs, kernel):
    depth_len = inputs.shape[2]
    padded = jnp.pad(inputs, ((0, 0), (0, 0), (1, 1), (0, 0)))
    summed = jnp.zeros(inputs.shape, jnp.float32)
    for depth_tap in range(3):
        summed = (
            summed
            + kernel[:, depth_tap][:, None, None, None]
            * padded[:, :, depth_tap : depth_tap + depth_len, :]
        )
    return summed


def mix_channels(weights, inputs):
    channels = inputs.shape[0]
    flat = inputs.reshape(channels, -1)
    return jnp.dot(weights, flat, preferred_element_type=jnp.float32).reshape(inputs.shape)


def forward_block(inputs, kernel_xy, kernel_z, weights):
    planar = conv_plane(inputs, kernel_xy)
    axial = conv_depth(planar, kernel_z).astype(jnp.bfloat16)
    preact = mix_channels(weights, axial)
    return (planar, axial, preact)


def silu_slope(preact):
    sigma = jax.nn.sigmoid(preact)
    return sigma * (1.0 + preact * (1.0 - sigma))


def backward_block(grad_out, planar, axial, preact, around, kernel_z, weights, trim):
    grad_pre = (grad_out.astype(jnp.float32) * silu_slope(preact)).astype(jnp.bfloat16)
    channels = grad_pre.shape[0]
    grad_axial = jnp.dot(
        weights.T, grad_pre.reshape(channels, -1), preferred_element_type=jnp.float32
    ).reshape(grad_pre.shape)
    grad_planar = conv_depth(grad_axial, kernel_z[:, ::-1]).astype(jnp.bfloat16)
    extent = grad_pre.shape[1]
    own_extent = extent - 2 * trim
    own_pre = grad_pre.reshape(channels, -1)
    own_axial = axial.reshape(channels, -1)
    grad_weights = lax.dot_general(
        own_pre, own_axial, (((1,), (1,)), ((), ())), preferred_element_type=jnp.float32
    )
    depth_len = planar.shape[2]
    planar_pad = jnp.pad(planar, ((0, 0), (0, 0), (1, 1), (0, 0)))
    grad_kz = jnp.stack(
        [
            jnp.sum(
                grad_axial * planar_pad[:, :, depth_tap : depth_tap + depth_len, :], axis=(1, 2, 3)
            )
            for depth_tap in range(3)
        ],
        axis=1,
    )
    own_grad_planar = grad_planar.astype(jnp.float32)
    across = around.shape[3]
    around_pad = jnp.pad(around, ((0, 0), (0, 0), (0, 0), (1, 1)))
    rows_list = []
    for row_tap in range(3):
        cols_list = []
        for col_tap in range(3):
            cols_list.append(
                jnp.sum(
                    own_grad_planar
                    * around_pad[
                        :, row_tap : row_tap + own_extent, :, col_tap : col_tap + across
                    ].astype(jnp.float32),
                    axis=(1, 2, 3),
                )
            )
        rows_list.append(jnp.stack(cols_list, axis=1))
    grad_kxy = jnp.stack(rows_list, axis=1)
    return (grad_planar, (grad_weights, grad_kxy, grad_kz))


def edge_grads(grad_planar):
    return padded_2(grad_planar, (("sp", 1),), 1)


def settle_all(lower, upper):
    summed = lax.psum((lower[0], lower[1], lower[2], upper[0], upper[1], upper[2]), ("sp", "dp"))
    return ((summed[0], summed[1], summed[2]), (summed[3], summed[4], summed[5]))


def on_device(volume, cotangent, kernels_xy, kernels_z, mixing):
    inputs = volume[0]
    grad_top = cotangent[0]
    kernel_xy = kernels_xy.astype(jnp.float32)
    kernel_z = kernels_z.astype(jnp.float32)
    slab_len = inputs.shape[1]
    ranks = lax.axis_size("sp")
    place = lax.axis_index("sp")
    wide = padded_2(inputs, (("sp", 1),), 2)
    planar1, axial1, preact1 = forward_block(wide, kernel_xy[0], kernel_z[0], mixing[0])
    hidden = jax.nn.silu(preact1).astype(jnp.bfloat16)
    spots = place * slab_len - 1 + jnp.arange(slab_len + 2, dtype=jnp.int32)
    hidden = jnp.where(
        ((spots >= 0) & (spots < slab_len * ranks))[None, :, None, None],
        hidden,
        jnp.zeros_like(hidden),
    )
    planar2, axial2, preact2 = forward_block(hidden, kernel_xy[1], kernel_z[1], mixing[1])
    grad_planar2, upper = backward_block(
        grad_top, planar2, axial2, preact2, hidden, kernel_z[1], mixing[1], 0
    )
    grad_hidden = conv_plane(edge_grads(grad_planar2), kernel_xy[1][:, ::-1, ::-1]).astype(
        jnp.bfloat16
    )
    grad_planar1, lower = backward_block(
        grad_hidden,
        planar1[:, 1:-1],
        axial1[:, 1:-1],
        preact1[:, 1:-1],
        wide[:, 1:-1],
        kernel_z[0],
        mixing[0],
        0,
    )
    grad_inputs = conv_plane(edge_grads(grad_planar1), kernel_xy[0][:, ::-1, ::-1]).astype(
        jnp.bfloat16
    )
    lower, upper = settle_all(lower, upper)
    factor = 1.0 / math.sqrt(
        lax.axis_size("dp") * slab_len * ranks * inputs.shape[2] * inputs.shape[3]
    )
    mixing_grad = jnp.stack([lower[0], upper[0]]) * factor
    xy_grad = jnp.stack([lower[1], upper[1]]) * factor
    z_grad = jnp.stack([lower[2], upper[2]]) * factor
    return (grad_inputs[None], mixing_grad, xy_grad, z_grad)


def solution(mesh):
    return jax.shard_map(
        on_device,
        mesh=mesh,
        in_specs=(P("dp", None, "sp", None, None), P("dp", None, "sp", None, None), P(), P(), P()),
        out_specs=(P("dp", None, "sp", None, None), P(), P(), P()),
        check_vma=False,
    )
```

profile of v0, /device:TPU:1, one launch (start us, length us, event | category | flops | bytes accessed | tf_op | source)
XLA Modules:
  0.0 328.5 jit_solution(12075035630448840751)
XLA Ops:
  7.2 1.5 copy.76
  8.8 4.9 %collective-permute-start = (bf16[96,2,8,128]{3,0,2,1:T(8,128)(2,1)S(1)}, bf16[96,2,8,128]{3,0,2,1:T(8,128)(2,1)S(1)}, u32[]{:S(2)}, u32[]{:S(2)}) collective-permute-start(bf16[96,2,8,128]{3,0,2,1:T(8,128)(2,1)S(1)} %get-tuple-element.61), channel_id=1, source_target_pairs={{0,4},{4,8},{8,12},{12,16},{16,20},{20,24},{24,28},{28,32},{32,36}... | collective-permute-start | bytes 1179656 | tf_op jit(solution)/shard_map/ppermute | solution.py:15
  13.8 1.9 collective-permute-start.1
  15.8 1.5 reshape.101
  18.5 4.4 %collective-permute-done.1 = bf16[96,2,8,128]{3,0,2,1:T(8,128)(2,1)S(1)} collective-permute-done((bf16[96,2,8,128]{3,0,2,1:T(8,128)(2,1)S(1)}, bf16[96,2,8,128]{3,0,2,1:T(8,128)(2,1)S(1)}, u32[]{:S(2)}, u32[]{:S(2)}) %collective-permute-start.1) | collective-permute-done | bytes 393248 | tf_op jit(solution)/shard_map/ppermute | solution.py:16
  23.0 3.1 multiply_add_fusion
  26.1 1.4 copy-done
  30.4 3.0 fusion.24
  36.5 6.6 %multiply_reduce_fusion.2 = (f32[96]{0:T(128)S(1)}, f32[96]{0:T(128)S(1)}, f32[96]{0:T(128)S(1)}, f32[96]{0:T(128)S(1)}, f32[96]{0:T(128)S(1)}, /*index=5*/f32[9...) fusion(f32[96,4,8,128]{3,2,1,0:T(8,128)S(1)} %bitcast.196, ...), kind=kLoop, calls=%fused_computation.147 | loop fusion | flops 15727488 | bytes 7477248 | tf_op jit(solution)/shard_map/reduce_sum | solution.py:83
  43.1 1.9 collective-permute-start.2
  45.1 2.6 collective-permute-start.3
  49.8 1.2 convolution_bitcast_fusion.3
  51.0 1.4 collective-permute-done.3
  52.3 1.5 fusion.9
  53.9 3.5 %multiply_convert_fusion.1 = bf16[96,4,8,128]{3,2,1,0:T(8,128)(2,1)S(1)} fusion(f32[96,6,8,128]{3,2,1,0:T(8,128)S(1)} %bitcast.193, bf16[96,6,8,130]{3,2,1,0:T(8,128)(2,1)S(1)} %fusion.9, f32[96]{0:T(128)S(1)} %get-tuple-element.71, bf16[96,1,8,128]{3,2,1,0:T(8,128)(2,1)S(1)} %collective-permute-done.3, bf16[96,4,8,128]{3,2,1,0:T(8,128)(2,1)S(1)} %get-tuple-element.56, ...), kind=kLoop, calls=%fused_computation.149 | loop fusion | flops 15335424 | bytes 8260992 | tf_op jit(solution)/shard_map/convert_element_type | solution.py:66
  60.7 1.4 fusion.31
  62.7 2.8 fusion.60
  66.2 2.1 collective-permute-start.4
  68.3 2.3 collective-permute-start.5
  70.6 242.2 %all-reduce.13.cloned.1.call-done = (f32[1,96,96]{2,1,0:T(8,128)}, f32[1,96,96]{2,1,0:T(8,128)}, f32[1,96,3,3]{1,3,2,0:T(4,128)}, f32[1,96,3,3]{1,3,2,0:T(4,128)...) async-done(((f32[1,96,96]{2,1,0:T(8,128)}, f32[1,96,96]{2,1,0:T(8,128)}, f32[1,96,3,3]{1,3,2,0:T(4,128)}, f32[1,96,3,3]{1,3,2,0:T(4,128)}, f32[1,96,3]{1,2,0:T(4,128)}, ...) | async-done | bytes 82960 | tf_op jit(solution)/shard_map/psum | solution.py:116
  315.4 1.5 maximum_multiply_fusion
  316.9 1.6 fusion.11
  318.4 2.0 fusion.92
  320.4 1.2 copy.31
  (68 shorter events, 16.6 us)
Async XLA Ops:
  7.2 8.5 %copy-start.7 = (bf16[2,96,3,3]{1,0,3,2:T(2,128)(2,1)S(1)}, bf16[2,96,3,3]{1,0,3,2:T(2,128)(2,1)}, u32[]{:S(2)}) copy-start(bf16[2,96,3,3]{1,0,3,2:T(2,128)(2,1)} %param.7) | copy-start | bytes 10372
  7.2 8.6 %copy-start.8 = (bf16[2,96,3]{1,0,2:T(2,128)(2,1)S(1)}, bf16[2,96,3]{1,0,2:T(2,128)(2,1)}, u32[]{:S(2)}) copy-start(bf16[2,96,3]{1,0,2:T(2,128)(2,1)} %param.8) | copy-start | bytes 3460
  7.2 8.6 %copy-start.4 = (bf16[1,96,4,8,128]{4,3,2,1,0:T(8,128)(2,1)S(1)}, bf16[1,96,4,8,128]{4,3,2,1,0:T(8,128)(2,1)}, u32[]{:S(2)}) copy-start(bf16[1,96,4,8,128]{4,3,2,1,0:T(8,128)(2,1)} %param.6) | copy-start | bytes 2359300
  7.2 305.6 %all-reduce.13.cloned.1.call-start = ((), (), s32[]{:S(2)}) async-start(), calls=%async_computation | async-start | bytes 229376 | tf_op jit(solution)/shard_map/psum | solution.py:116
  8.8 9.6 %collective-permute-start = (bf16[96,2,8,128]{3,0,2,1:T(8,128)(2,1)S(1)}, bf16[96,2,8,128]{3,0,2,1:T(8,128)(2,1)S(1)}, u32[]{:S(2)}, u32[]{:S(2)}) collective-permute-start(bf16[96,2,8,128]{3,0,2,1:T(8,128)(2,1)S(1)} %get-tuple-element.61), channel_id=1, source_target_pairs={{0,4},{4,8},{8,12},{12,16},{16,20},{20,24},{24,28},{28,32},{32,36}... | collective-permute-start | bytes 1179656 | tf_op jit(solution)/shard_map/ppermute | solution.py:15
  13.8 9.1 %collective-permute-start.1 = (bf16[96,2,8,128]{3,0,2,1:T(8,128)(2,1)S(1)}, bf16[96,2,8,128]{3,0,2,1:T(8,128)(2,1)S(1)}, u32[]{:S(2)}, u32[]{:S(2)}) collective-permute-start(bf16[96,2,8,128]{3,0,2,1:T(8,128)(2,1)S(1)} %get-tuple-element.62), channel_id=1, source_target_pairs={{4,0},{8,4},{12,8},{16,12},{20,16},{24,20},{28,24},{32,28},{36,32}... | collective-permute-start | bytes 1179656 | tf_op jit(solution)/shard_map/ppermute | solution.py:16
  23.0 3.1 copy-start.2
  26.1 1.4 copy-start
  28.1 0.8 copy-start.6
  34.0 1.4 copy-start.5
  43.1 7.8 %collective-permute-start.2 = (bf16[96,1,8,128]{3,2,1,0:T(8,128)(2,1)S(1)}, bf16[96,1,8,128]{3,2,1,0:T(8,128)(2,1)S(1)}, u32[]{:S(2)}, u32[]{:S(2)}) collective-permute-start(bf16[96,1,8,128]{3,2,1,0:T(8,128)(2,1)S(1)} %get-tuple-element.59), channel_id=1, source_target_pairs={{0,4},{4,8},{8,12},{12,16},{16,20},{20,24},{24,28},{28,32},{32,36}... | collective-permute-start | bytes 589832 | tf_op jit(solution)/shard_map/ppermute | solution.py:15
  45.1 7.3 %collective-permute-start.3 = (bf16[96,1,8,128]{3,2,1,0:T(8,128)(2,1)S(1)}, bf16[96,1,8,128]{3,2,1,0:T(8,128)(2,1)S(1)}, u32[]{:S(2)}, u32[]{:S(2)}) collective-permute-start(bf16[96,1,8,128]{3,2,1,0:T(8,128)(2,1)S(1)} %get-tuple-element.60), channel_id=1, source_target_pairs={{4,0},{8,4},{12,8},{16,12},{20,16},{24,20},{28,24},{32,28},{36,32}... | collective-permute-start | bytes 589832 | tf_op jit(solution)/shard_map/ppermute | solution.py:16
  58.5 1.7 copy-start.1
  58.9 1.8 slice-start
  60.7 2.0 slice-start.1
  60.7 2.0 copy-start.3
  66.2 250.6 %collective-permute-start.4 = (bf16[96,1,8,128]{3,0,2,1:T(8,128)(2,1)S(1)}, bf16[96,1,8,128]{3,0,2,1:T(8,128)(2,1)S(1)}, u32[]{:S(2)}, u32[]{:S(2)}) collective-permute-start(bf16[96,1,8,128]{3,0,2,1:T(8,128)(2,1)S(1)} %get-tuple-element.57), channel_id=1, source_target_pairs={{0,4},{4,8},{8,12},{12,16},{16,20},{20,24},{24,28},{28,32},{32,36}... | collective-permute-start | bytes 589832 | tf_op jit(solution)/shard_map/ppermute | solution.py:15
  68.3 248.6 %collective-permute-start.5 = (bf16[96,1,8,128]{3,0,2,1:T(8,128)(2,1)S(1)}, bf16[96,1,8,128]{3,0,2,1:T(8,128)(2,1)S(1)}, u32[]{:S(2)}, u32[]{:S(2)}) collective-permute-start(bf16[96,1,8,128]{3,0,2,1:T(8,128)(2,1)S(1)} %get-tuple-element.58), channel_id=1, source_target_pairs={{4,0},{8,4},{12,8},{16,12},{20,16},{24,20},{28,24},{32,28},{36,32}... | collective-permute-start | bytes 589832 | tf_op jit(solution)/shard_map/ppermute | solution.py:16
Sparse Core Ops, SparseCore 0:
  66.3 246.4 all-reduce.12
where the time goes:
time: 329 us; the launch traced here: 328 us
  waiting for transfers between devices  249 us (76%)
  other arithmetic  33.4 us (10%)
  starting transfers between devices  15.7 us (5%)
  between operations  14.4 us (4%)
  local copies, waits for them, and re-layouts  11.5 us (3%)
  matrix products  4.28 us (1%)
    psum x1, waiting for transfers between devices, settle_all(): lax.psum((lower[0], lower[1], lower[2], upper[0], upper[1], upper[2]), ('...  242 us
    ppermute x3, starting transfers between devices, padded_2(): before = lax.ppermute(last, axis, up)  8.92 us
    unnamed x28, local copies, waits for them, and re-layouts  8.82 us
    reduce_sum x2, other arithmetic, backward_block(): jnp.sum(grad_axial * planar_pad[:, :, depth_tap:depth_tap + depth_len, :]...  7.96 us
    ppermute x3, starting transfers between devices, padded_2(): after = lax.ppermute(first, axis, down)  6.79 us
  transfers between devices with their start and end apart: 7, of which 4 were waited for; matrix products, arithmetic and copies ran while one was open for 3% of the time, Pallas kernels for 0%

commit v1 on v0

--- a/solution.py
+++ b/solution.py
@@ -113,7 +113,9 @@
 
 
 def settle_all(lower, upper):
-    summed = lax.psum((lower[0], lower[1], lower[2], upper[0], upper[1], upper[2]), ("sp", "dp"))
+    summed = lax.psum(
+        lax.psum((lower[0], lower[1], lower[2], upper[0], upper[1], upper[2]), "dp"), "sp"
+    )
     return ((summed[0], summed[1], summed[2]), (summed[3], summed[4], summed[5]))
 
 

time: 329 us -> 310 us (0.942)
  waiting for transfers between devices: 249 us -> 227 us
  starting transfers between devices: 15.7 us -> 19.3 us
    psum x1 -> x2, waiting for transfers between devices: 242 us -> 220 us  [the longest x1 173 us: settle_all(): lax.psum(lax.psum((lower[0], lower[1], lower[2], upper[0], upper[1], uppe...]
    ppermute x3, starting transfers between devices: 8.92 us -> 12.8 us  [padded_2(): before = lax.ppermute(last, axis, up)]
  transfers between devices with their start and end apart: 7 -> 8, of which waited for: 4 -> 5; matrix products, arithmetic and copies ran while one was open for 3% -> 3% of each run, Pallas kernels for 0% -> 0%
where the time goes in v1:
time: 310 us
  waiting for transfers between devices  227 us (73%)
  other arithmetic  33.3 us (11%)
  starting transfers between devices  19.3 us (6%)
  between operations  14.5 us (5%)
  local copies, waits for them, and re-layouts  11.5 us (4%)
  matrix products  4.28 us (1%)
    psum x1, waiting for transfers between devices, settle_all(): lax.psum(lax.psum((lower[0], lower[1], lower[2], upper[0], upper[1], uppe...  173 us
    psum x1, waiting for transfers between devices, settle_all(): lax.psum((lower[0], lower[1], lower[2], upper[0], upper[1], upper[2]), 'dp')  47.1 us
    ppermute x3, starting transfers between devices, padded_2(): before = lax.ppermute(last, axis, up)  12.8 us
    unnamed x28, local copies, waits for them, and re-layouts  8.82 us
    reduce_sum x2, other arithmetic, backward_block(): jnp.sum(grad_axial * planar_pad[:, :, depth_tap:depth_tap + depth_len, :]...  7.96 us
    ppermute x3, starting transfers between devices, padded_2(): after = lax.ppermute(first, axis, down)  6.44 us
  transfers between devices with their start and end apart: 8, of which 5 were waited for; matrix products, arithmetic and copies ran while one was open for 3% of the time, Pallas kernels for 0%

profile of v1, /device:TPU:1, one launch (start us, length us, event | category | flops | bytes accessed | tf_op | source)
XLA Modules:
  0.0 309.6 jit_solution(15040629994780435620)
XLA Ops:
  7.2 1.5 copy.76
  8.8 4.9 %collective-permute-start = (bf16[96,2,8,128]{3,0,2,1:T(8,128)(2,1)S(1)}, bf16[96,2,8,128]{3,0,2,1:T(8,128)(2,1)S(1)}, u32[]{:S(2)}, u32[]{:S(2)}) collective-permute-start(bf16[96,2,8,128]{3,0,2,1:T(8,128)(2,1)S(1)} %get-tuple-element.67), channel_id=1, source_target_pairs={{0,4},{4,8},{8,12},{12,16},{16,20},{20,24},{24,28},{28,32},{32,36}... | collective-permute-start | bytes 1179656 | tf_op jit(solution)/shard_map/ppermute | solution.py:15
  13.8 1.9 collective-permute-start.1
  15.8 1.5 reshape.101
  18.5 4.4 %collective-permute-done.1 = bf16[96,2,8,128]{3,0,2,1:T(8,128)(2,1)S(1)} collective-permute-done((bf16[96,2,8,128]{3,0,2,1:T(8,128)(2,1)S(1)}, bf16[96,2,8,128]{3,0,2,1:T(8,128)(2,1)S(1)}, u32[]{:S(2)}, u32[]{:S(2)}) %collective-permute-start.1) | collective-permute-done | bytes 393248 | tf_op jit(solution)/shard_map/ppermute | solution.py:16
  23.0 3.1 multiply_add_fusion
  26.1 1.4 copy-done
  30.4 3.0 fusion.24
  36.5 6.6 %multiply_reduce_fusion.2 = (f32[96]{0:T(128)S(1)}, f32[96]{0:T(128)S(1)}, f32[96]{0:T(128)S(1)}, f32[96]{0:T(128)S(1)}, f32[96]{0:T(128)S(1)}, /*index=5*/f32[9...) fusion(f32[96,4,8,128]{3,2,1,0:T(8,128)S(1)} %bitcast.190, ...), kind=kLoop, calls=%fused_computation.147 | loop fusion | flops 15727488 | bytes 7477248 | tf_op jit(solution)/shard_map/reduce_sum | solution.py:83
  43.1 1.9 collective-permute-start.2
  45.1 2.6 collective-permute-start.3
  51.0 1.4 collective-permute-done.3
  52.3 1.5 fusion.9
  53.9 3.5 %multiply_convert_fusion.1 = bf16[96,4,8,128]{3,2,1,0:T(8,128)(2,1)S(1)} fusion(f32[96,6,8,128]{3,2,1,0:T(8,128)S(1)} %bitcast.187, bf16[96,6,8,130]{3,2,1,0:T(8,128)(2,1)S(1)} %fusion.9, f32[96]{0:T(128)S(1)} %get-tuple-element.77, bf16[96,1,8,128]{3,2,1,0:T(8,128)(2,1)S(1)} %collective-permute-done.3, bf16[96,4,8,128]{3,2,1,0:T(8,128)(2,1)S(1)} %get-tuple-element.62, ...), kind=kLoop, calls=%fused_computation.149 | loop fusion | flops 15335424 | bytes 8260992 | tf_op jit(solution)/shard_map/convert_element_type | solution.py:66
  60.7 1.4 fusion.31
  62.7 2.8 fusion.60
  66.2 47.1 %all-reduce.17.cloned.1.call-done = (f32[96,96]{1,0:T(8,128)}, f32[96,96]{1,0:T(8,128)}, f32[96,3,3]{0,2,1:T(4,128)}, f32[96,3,3]{0,2,1:T(4,128)}, f32[96,3]{0,1:T(4,128)}, /*index=5*/f32[96,3]{0,1:T(4,128)}) async-done(((f32[96,96]{1,0:T(8,128)}, f32[96,96]{1,0:T(8,128)}, f32[96,3,3]{0,2,1:T(4,128)}, f32[96,3,3]{0,2,1:T(4,128)}, f32[96,3]{0,1:T(4,128)}, /*index=5*/f32[96,3]{0,1:T(4,128)}), ...) | async-done | bytes 82960 | tf_op jit(solution)/shard_map/psum | solution.py:117
  113.4 5.9 %collective-permute-start.4 = (bf16[96,1,8,128]{3,0,2,1:T(8,128)(2,1)S(1)}, bf16[96,1,8,128]{3,0,2,1:T(8,128)(2,1)S(1)}, u32[]{:S(2)}, u32[]{:S(2)}) collective-permute-start(bf16[96,1,8,128]{3,0,2,1:T(8,128)(2,1)S(1)} %get-tuple-element.63), channel_id=1, source_target_pairs={{0,4},{4,8},{8,12},{12,16},{16,20},{20,24},{24,28},{28,32},{32,36}... | collective-permute-start | bytes 589832 | tf_op jit(solution)/shard_map/ppermute | solution.py:15
  119.3 1.9 collective-permute-start.5
  121.2 172.8 %all-reduce.15.cloned.1.call-done = (f32[1,96,96]{2,1,0:T(8,128)}, f32[1,96,96]{2,1,0:T(8,128)}, f32[1,96,3,3]{1,3,2,0:T(4,128)}, f32[1,96,3,3]{1,3,2,0:T(4,128)...) async-done(((f32[1,96,96]{2,1,0:T(8,128)}, f32[1,96,96]{2,1,0:T(8,128)}, f32[1,96,3,3]{1,3,2,0:T(4,128)}, f32[1,96,3,3]{1,3,2,0:T(4,128)}, f32[1,96,3]{1,2,0:T(4,128)}, ...) | async-done | bytes 82960 | tf_op jit(solution)/shard_map/psum | solution.py:116
  296.6 1.5 maximum_multiply_fusion
  298.0 1.6 fusion.11
  299.6 2.0 fusion.92
  301.6 1.2 copy.31
  (71 shorter events, 17.8 us)
Async XLA Ops:
  7.2 8.5 %copy-start.7 = (bf16[2,96,3,3]{1,0,3,2:T(2,128)(2,1)S(1)}, bf16[2,96,3,3]{1,0,3,2:T(2,128)(2,1)}, u32[]{:S(2)}) copy-start(bf16[2,96,3,3]{1,0,3,2:T(2,128)(2,1)} %param.7) | copy-start | bytes 10372
  7.2 8.6 %copy-start.8 = (bf16[2,96,3]{1,0,2:T(2,128)(2,1)S(1)}, bf16[2,96,3]{1,0,2:T(2,128)(2,1)}, u32[]{:S(2)}) copy-start(bf16[2,96,3]{1,0,2:T(2,128)(2,1)} %param.8) | copy-start | bytes 3460
  7.2 8.6 %copy-start.4 = (bf16[1,96,4,8,128]{4,3,2,1,0:T(8,128)(2,1)S(1)}, bf16[1,96,4,8,128]{4,3,2,1,0:T(8,128)(2,1)}, u32[]{:S(2)}) copy-start(bf16[1,96,4,8,128]{4,3,2,1,0:T(8,128)(2,1)} %param.6) | copy-start | bytes 2359300
  7.2 106.1 %all-reduce.17.cloned.1.call-start = ((), (), s32[]{:S(2)}) async-start(), calls=%async_computation.1 | async-start | bytes 229376 | tf_op jit(solution)/shard_map/psum | solution.py:117
  8.8 9.6 %collective-permute-start = (bf16[96,2,8,128]{3,0,2,1:T(8,128)(2,1)S(1)}, bf16[96,2,8,128]{3,0,2,1:T(8,128)(2,1)S(1)}, u32[]{:S(2)}, u32[]{:S(2)}) collective-permute-start(bf16[96,2,8,128]{3,0,2,1:T(8,128)(2,1)S(1)} %get-tuple-element.67), channel_id=1, source_target_pairs={{0,4},{4,8},{8,12},{12,16},{16,20},{20,24},{24,28},{28,32},{32,36}... | collective-permute-start | bytes 1179656 | tf_op jit(solution)/shard_map/ppermute | solution.py:15
  13.8 9.1 %collective-permute-start.1 = (bf16[96,2,8,128]{3,0,2,1:T(8,128)(2,1)S(1)}, bf16[96,2,8,128]{3,0,2,1:T(8,128)(2,1)S(1)}, u32[]{:S(2)}, u32[]{:S(2)}) collective-permute-start(bf16[96,2,8,128]{3,0,2,1:T(8,128)(2,1)S(1)} %get-tuple-element.68), channel_id=1, source_target_pairs={{4,0},{8,4},{12,8},{16,12},{20,16},{24,20},{28,24},{32,28},{36,32}... | collective-permute-start | bytes 1179656 | tf_op jit(solution)/shard_map/ppermute | solution.py:16
  23.0 3.1 copy-start.2
  26.1 1.4 copy-start
  28.1 0.8 copy-start.6
  34.0 1.4 copy-start.5
  43.1 7.8 %collective-permute-start.2 = (bf16[96,1,8,128]{3,2,1,0:T(8,128)(2,1)S(1)}, bf16[96,1,8,128]{3,2,1,0:T(8,128)(2,1)S(1)}, u32[]{:S(2)}, u32[]{:S(2)}) collective-permute-start(bf16[96,1,8,128]{3,2,1,0:T(8,128)(2,1)S(1)} %get-tuple-element.65), channel_id=1, source_target_pairs={{0,4},{4,8},{8,12},{12,16},{16,20},{20,24},{24,28},{28,32},{32,36}... | collective-permute-start | bytes 589832 | tf_op jit(solution)/shard_map/ppermute | solution.py:15
  45.1 7.3 %collective-permute-start.3 = (bf16[96,1,8,128]{3,2,1,0:T(8,128)(2,1)S(1)}, bf16[96,1,8,128]{3,2,1,0:T(8,128)(2,1)S(1)}, u32[]{:S(2)}, u32[]{:S(2)}) collective-permute-start(bf16[96,1,8,128]{3,2,1,0:T(8,128)(2,1)S(1)} %get-tuple-element.66), channel_id=1, source_target_pairs={{4,0},{8,4},{12,8},{16,12},{20,16},{24,20},{28,24},{32,28},{36,32}... | collective-permute-start | bytes 589832 | tf_op jit(solution)/shard_map/ppermute | solution.py:16
  58.5 1.7 copy-start.1
  58.9 1.8 slice-start
  60.7 2.0 slice-start.1
  60.7 2.0 copy-start.3
  66.1 227.8 %all-reduce.15.cloned.1.call-start = ((), (), s32[]{:S(2)}) async-start(), calls=%async_computation | async-start | bytes 229376 | tf_op jit(solution)/shard_map/psum | solution.py:116
  113.4 184.7 %collective-permute-start.4 = (bf16[96,1,8,128]{3,0,2,1:T(8,128)(2,1)S(1)}, bf16[96,1,8,128]{3,0,2,1:T(8,128)(2,1)S(1)}, u32[]{:S(2)}, u32[]{:S(2)}) collective-permute-start(bf16[96,1,8,128]{3,0,2,1:T(8,128)(2,1)S(1)} %get-tuple-element.63), channel_id=1, source_target_pairs={{0,4},{4,8},{8,12},{12,16},{16,20},{20,24},{24,28},{28,32},{32,36}... | collective-permute-start | bytes 589832 | tf_op jit(solution)/shard_map/ppermute | solution.py:15
  119.3 178.8 %collective-permute-start.5 = (bf16[96,1,8,128]{3,0,2,1:T(8,128)(2,1)S(1)}, bf16[96,1,8,128]{3,0,2,1:T(8,128)(2,1)S(1)}, u32[]{:S(2)}, u32[]{:S(2)}) collective-permute-start(bf16[96,1,8,128]{3,0,2,1:T(8,128)(2,1)S(1)} %get-tuple-element.64), channel_id=1, source_target_pairs={{4,0},{8,4},{12,8},{16,12},{20,16},{24,20},{28,24},{32,28},{36,32}... | collective-permute-start | bytes 589832 | tf_op jit(solution)/shard_map/ppermute | solution.py:16
Sparse Core Ops, SparseCore 0:
  66.3 47.0 all-reduce.16
  118.1 175.7 all-reduce.14
